TPU v7x, 128 devices: a whole 4x4x4 slice. The times are simulated.
128 devices in a mesh: grp: 8 (over y, core), nbr: 16 (over x, z).
Axes of the slice: x: 4, y: 4, z: 4, core: 2. Of those that a mesh axis runs over, the one named last changes fastest.
Arguments:
- sims: float32 [2048, 128, 128], P(('grp', 'nbr')), may hold values from -6 to 6
- own_tiles: float32 [24576, 128, 128], P(('grp', 'nbr')), may hold values from -0.15625 to 0.15625
- own_cols: int32 [24576], P(('grp', 'nbr')), may hold values from 0 to 271
- own_rows: int32 [24576], P(('grp', 'nbr')), may hold values from 0 to 15
- help_tiles: float32 [4096, 128, 128], P(('grp', 'nbr')), may hold values from -0.15625 to 0.15625
- help_cols: int32 [4096], P(('grp', 'nbr')), may hold values from 0 to 271
- help_rows: int32 [4096], P(('grp', 'nbr')), may hold values from 0 to 15
- help_live: int32 [4096], P(('grp', 'nbr')), may hold values from 0 to 1, as said below
Outputs:
- reobserved: float32 [2048, 128, 128], P(('grp', 'nbr'))
Inputs may be any that keep to these rules, and one draw needn't show every extreme that they name: `help_live`: helper slot j of a device serves the owner of neighbour index j // 2 in the same group, so at most 2 live slots go from one device to one owner; in every group one owner receives all 2 slots live from every device of the group.
All inputs are finite; a program needn't handle non-finite values.
Results may differ from a plain program's by a relative error of at most 0.0001.
Values sent between devices are 32-bit elements; how exact they have to be, the bound alone decides.
A program may use at most 192 MiB of HBM per device.

v0:
```python
import jax
import jax.numpy as jnp
from jax import lax
from jax.sharding import PartitionSpec as P

RIM = 8


def padded(shard, sides, width):
    for axis, dim in sides:
        peers, length = (lax.axis_size(axis), shard.shape[dim])
        up = [(i, (i + 1) % peers) for i in range(peers - 1)]
        down = [(j, i) for i, j in up]
        last = lax.slice_in_dim(shard, length - width, length, axis=dim)
        initial = lax.slice_in_dim(shard, 0, width, axis=dim)
        before = lax.ppermute(last, axis, up)
        after = lax.ppermute(initial, axis, down)
        shard = jnp.concatenate([before, shard, after], axis=dim)
    return shard


def pick_from(source, first, cols):
    length = source.shape[0]
    index = cols - first
    valid = ((index >= 0) & (index < length)).astype(jnp.float32)
    taken = jnp.take(source, jnp.clip(index, 0, length - 1), axis=0)
    return taken * valid[:, None, None]


def local(sims, own_tiles, own_cols, own_rows, help_tiles, help_cols, help_rows, help_live):
    high = lax.Precision.HIGHEST
    rows_dev = sims.shape[0]
    neighbours = lax.axis_size("nbr")
    group_rows = rows_dev * neighbours
    help_dev = help_tiles.shape[0]
    slots_owner = help_dev // neighbours
    group = lax.all_gather(sims, "nbr", axis=0, tiled=True)
    own_pick = pick_from(group, RIM, own_cols)
    help_pick = pick_from(group, RIM, help_cols)
    edges = jnp.concatenate([group[:RIM], group[group_rows - RIM :]], axis=0)
    rims = padded(edges, (("grp", 0),), RIM)
    lower = rims[:RIM]
    upper = rims[rims.shape[0] - RIM :]
    own_pick = (
        own_pick + pick_from(lower, 0, own_cols) + pick_from(upper, RIM + group_rows, own_cols)
    )
    help_pick = (
        help_pick + pick_from(lower, 0, help_cols) + pick_from(upper, RIM + group_rows, help_cols)
    )
    own_terms = jnp.einsum("tij,tjs->tis", own_tiles, own_pick, precision=high)
    select = (own_rows[None, :] == jnp.arange(rows_dev, dtype=jnp.int32)[:, None]).astype(
        jnp.float32
    )
    own_sum = jnp.einsum("rt,tis->ris", select, own_terms, precision=high)
    help_terms = (
        jnp.einsum("tij,tjs->tis", help_tiles, help_pick, precision=high)
        * help_live.astype(jnp.float32)[:, None, None]
    )
    outgoing = help_terms.reshape(neighbours, slots_owner, help_terms.shape[1], help_terms.shape[2])
    out_rows = help_rows.astype(jnp.float32).reshape(neighbours, slots_owner)
    incoming, in_rows = (
        lax.all_to_all(outgoing, "nbr", split_axis=0, concat_axis=0, tiled=True),
        lax.all_to_all(out_rows, "nbr", split_axis=0, concat_axis=0, tiled=True),
    )
    flat_terms = incoming.reshape(help_dev, incoming.shape[2], incoming.shape[3])
    flat_rows = in_rows.reshape(help_dev)
    picker = (flat_rows[None, :] == jnp.arange(rows_dev, dtype=jnp.float32)[:, None]).astype(
        jnp.float32
    )
    help_sum = jnp.einsum("rt,tis->ris", picker, flat_terms, precision=high)
    return own_sum + help_sum


def solution(mesh):
    placed = (
        P(("grp", "nbr"), None, None),
        P(("grp", "nbr"), None, None),
        P(("grp", "nbr")),
        P(("grp", "nbr")),
        P(("grp", "nbr"), None, None),
        P(("grp", "nbr")),
        P(("grp", "nbr")),
        P(("grp", "nbr")),
    )
    return jax.shard_map(
        local, mesh=mesh, in_specs=placed, out_specs=P(("grp", "nbr"), None, None), check_vma=False
    )
```

profile of v0, /device:TPU:1, one launch (start us, length us, event | category | flops | bytes accessed | tf_op | source)
XLA Modules:
  0.0 253.4 jit_solution(752253415979622065)
XLA Ops:
  6.5 0.0 copy-start
  6.5 0.0 copy-start.2
  6.5 0.0 copy-start.4
  6.5 0.0 all-gather.2.cloned.1.call-start
  6.5 0.7 all-gather.2.cloned.1.call-update
  7.3 0.7 convert_element_type.29
  7.9 0.7 all_to_all.9
  8.6 8.4 %all-to-all-start = ((f32[16,1,2]{2,1,0:T(1,128)}), f32[16,1,2]{2,1,0:T(1,128)S(1)}, u32[]{:S(2)}, u32[]{:S(2)}) async-start(f32[16,1,2]{2,1,0:T(1,128)} %bitcast.2), calls=%async_computation | async-start | bytes 16384 | tf_op jit(solution)/shard_map/all_to_all | solution.py:63
  17.0 0.7 compare_select_fusion.1
  17.7 0.7 and_convert_fusion.2
  18.4 105.5 %all-gather.2.cloned.1.call-done = f32[256,128,128]{2,1,0:T(8,128)} async-done(((f32[16,128,128]{2,1,0:T(8,128)}), f32[256,128,128]{2,1,0:T(8,128)}) %all-gather.2.cloned.1.call-update) | async-done | bytes 16777232 | tf_op jit(solution)/shard_map/all_gather | solution.py:37
  123.9 2.3 fusion.43
  126.1 3.8 %collective-permute-start = (f32[8,128,128]{2,1,0:T(8,128)}, f32[8,128,128]{2,1,0:T(8,128)S(1)}, u32[]{:S(2)}, u32[]{:S(2)}) collective-permute-start(f32[8,128,128]{2,1,0:T(8,128)} %get-tuple-element.17), channel_id=1, source_target_pairs={{0,16},{16,32},{32,48},{48,64},{64,80},{80,96},{96,112},{1,17},{17... | collective-permute-start | bytes 1572872 | tf_op jit(solution)/shard_map/ppermute | solution.py:16
  130.0 1.9 collective-permute-start.1
  131.9 0.0 copy-done.2
  132.0 0.0 copy-done.4
  132.0 0.0 all-to-all-done
  132.0 0.5 broadcast.82
  132.5 0.6 reduce.3
  133.1 0.1 eq.31
  133.2 7.7 %gather_fusion.1 = f32[32,128,128]{2,1,0:T(8,128)} fusion(f32[256,128,128]{2,1,0:T(8,128)} %all-gather.2.cloned.1.call-done, s32[1024]{0:T(1024)S(1)} %pad_clamp_fusion.2), kind=kCustom, calls=%fused_computation.5 | custom fusion | bytes 4194432 | tf_op jit(solution)/shard_map/jit(_take)/gather | solution.py:26
  140.9 16.5 %gather_fusion = f32[192,128,128]{2,1,0:T(8,128)} fusion(f32[256,128,128]{2,1,0:T(8,128)} %all-gather.2.cloned.1.call-done, s32[1024]{0:T(1024)S(1)} %get-tuple-element.37), kind=kCustom, calls=%fused_computation.4 | custom fusion | bytes 25166592 | tf_op jit(solution)/shard_map/jit(_take)/gather | solution.py:26
  157.4 0.0 collective-permute-done.1
  157.4 2.0 gather_fusion.5
  159.4 0.0 collective-permute-done
  159.4 2.0 gather_fusion.4
  161.4 0.0 copy-done
  161.4 8.3 %fusion.24 = f32[32,128,128]{2,1,0:T(8,128)} fusion(f32[32,128,128]{2,1,0:T(8,128)S(1)} %copy-done, f32[32,128,128]{2,1,0:T(8,128)} %gather_fusion.5, f32[32,128,128]{2,1,0:T(8,128)} %gather_fusion.4, f32[32,128,128]{2,1,0:T(8,128)} %gather_fusion.1, f32[32]{0:T(128)S(1)} %convert_element_type.33, f32[32]{0:T(128)S(1)} %get-tuple-element.28, ...), kind=kOutput, calls=%fused_computation.28 | convolution fusion | flops 810024960 | bytes 10486368 | tf_op jit(solution)/shard_map/tij,tjs->tis/dot_general | solution.py:56
  169.8 5.0 %all-to-all-start.1 = ((f32[16,2,128,128]{2,3,1,0:T(8,128)}), f32[16,2,128,128]{2,3,1,0:T(8,128)S(1)}, u32[]{:S(2)}, u32[]{:S(2)}) async-start(f32[16,2,128,128]{2,3,1,0:T(8,128)} %bitcast.18), calls=%async_computation.1 | async-start | bytes 4194304 | tf_op jit(solution)/shard_map/all_to_all | solution.py:62
  174.8 5.9 %gather_fusion.2 = f32[192,128,128]{2,1,0:T(8,128)} fusion(f32[8,128,128]{2,1,0:T(8,128)S(1)} %collective-permute-done, s32[1024]{0:T(1024)S(1)} %pad_clamp_fusion.4), kind=kCustom, calls=%fused_computation.clone | custom fusion | bytes 25166592 | tf_op jit(solution)/shard_map/jit(_take)/gather | solution.py:26
  180.7 5.9 %gather_fusion.3 = f32[192,128,128]{2,1,0:T(8,128)} fusion(f32[8,128,128]{2,1,0:T(8,128)S(1)} %collective-permute-done.1, s32[1024]{0:T(1024)S(1)} %get-tuple-element.36), kind=kCustom, calls=%fused_computation.2.clone | custom fusion | bytes 25166592 | tf_op jit(solution)/shard_map/jit(_take)/gather | solution.py:26
  186.6 33.9 %fusion.14 = f32[192,128,128]{1,2,0:T(8,128)} fusion(f32[192,128,128]{2,1,0:T(8,128)} %param.13, f32[192,128,128]{2,1,0:T(8,128)} %gather_fusion.3, f32[192,128,128]{2,1,0:T(8,128)} %gather_fusion.2, f32[192,128,128]{2,1,0:T(8,128)} %gather_fusion, f32[192]{0:T(256)S(1)} %get-tuple-element.21, f32[192]{0:T(256)S(1)} %get-tuple-element.26, ...), kind=kOutput, calls=%fused_computation.20 | convolution fusion | flops 4857004032 | bytes 62917440 | tf_op jit(solution)/shard_map/tij,tjs->tis/dot_general | solution.py:50
  220.4 0.0 copy-start.3
  220.4 12.7 %copy.16 = f32[192,128,128]{2,0,1:T(8,128)} copy(f32[192,128,128]{1,2,0:T(8,128)} %fusion.14) | data formatting | bytes 25165824 | tf_op jit(solution)/shard_map/tij,tjs->tis/dot_general | solution.py:50
  233.2 0.0 copy-done.3
  233.2 7.1 %fusion.35 = f32[16,128,128]{2,0,1:T(8,128)S(1)} fusion(f32[192,128,128]{2,0,1:T(8,128)} %copy.16, s32[192]{0:T(256)S(1)} %copy-done.3), kind=kOutput, calls=%fused_computation.39 | convolution fusion | flops 603982848 | bytes 13632256 | tf_op jit(solution)/shard_map/rt,tis->ris/dot_general | solution.py:54
  240.2 0.0 all-to-all-done.1
  240.2 2.5 copy.19
  242.7 0.0 copy-start.1
  242.7 2.5 %convolution_add_fusion = f32[16,128,128]{2,0,1:T(8,128)S(1)} fusion(f32[16,128,128]{2,0,1:T(8,128)S(1)} %fusion.35, f32[32,128,128]{2,0,1:T(8,128)} %bitcast.17, f32[32]{0:T(128)S(1)} %eq.31), kind=kOutput, calls=%fused_computation.29 | convolution fusion | flops 100925952 | bytes 4194432 | tf_op jit(solution)/shard_map/rt,tis->ris/dot_general | solution.py:70
  245.2 1.3 copy.20
  246.5 0.0 copy-done.1
  (6 shorter events, 0.0 us)
Async XLA Ops:
  6.5 154.9 %copy-start = (f32[32,128,128]{2,1,0:T(8,128)S(1)}, f32[32,128,128]{2,1,0:T(8,128)}, u32[]{:S(2)}) copy-start(f32[32,128,128]{2,1,0:T(8,128)} %param.16) | copy-start | bytes 6291460
  6.5 125.4 %copy-start.2 = (s32[192]{0:T(256)S(1)}, s32[192]{0:T(256)}, u32[]{:S(2)}) copy-start(s32[192]{0:T(256)} %param.14) | copy-start | bytes 2308
  6.5 125.4 %copy-start.4 = (s32[32]{0:T(128)S(1)}, s32[32]{0:T(128)}, u32[]{:S(2)}) copy-start(s32[32]{0:T(128)} %param.19) | copy-start | bytes 388
  6.5 117.3 %all-gather.2.cloned.1.call-start = ((), (), s32[]{:S(2)}) async-start(), calls=%async_computation.2 | async-start | bytes 17825792 | tf_op jit(solution)/shard_map/all_gather | solution.py:37
  8.6 123.4 %all-to-all-start = ((f32[16,1,2]{2,1,0:T(1,128)}), f32[16,1,2]{2,1,0:T(1,128)S(1)}, u32[]{:S(2)}, u32[]{:S(2)}) async-start(f32[16,1,2]{2,1,0:T(1,128)} %bitcast.2), calls=%async_computation | async-start | bytes 16384 | tf_op jit(solution)/shard_map/all_to_all | solution.py:63
  126.1 33.3 %collective-permute-start = (f32[8,128,128]{2,1,0:T(8,128)}, f32[8,128,128]{2,1,0:T(8,128)S(1)}, u32[]{:S(2)}, u32[]{:S(2)}) collective-permute-start(f32[8,128,128]{2,1,0:T(8,128)} %get-tuple-element.17), channel_id=1, source_target_pairs={{0,16},{16,32},{32,48},{48,64},{64,80},{80,96},{96,112},{1,17},{17... | collective-permute-start | bytes 1572872 | tf_op jit(solution)/shard_map/ppermute | solution.py:16
  130.0 27.5 %collective-permute-start.1 = (f32[8,128,128]{2,1,0:T(8,128)}, f32[8,128,128]{2,1,0:T(8,128)S(1)}, u32[]{:S(2)}, u32[]{:S(2)}) collective-permute-start(f32[8,128,128]{2,1,0:T(8,128)} %get-tuple-element.18), channel_id=1, source_target_pairs={{16,0},{32,16},{48,32},{64,48},{80,64},{96,80},{112,96},{17,1},{33... | collective-permute-start | bytes 1572872 | tf_op jit(solution)/shard_map/ppermute | solution.py:17
  169.8 70.5 %all-to-all-start.1 = ((f32[16,2,128,128]{2,3,1,0:T(8,128)}), f32[16,2,128,128]{2,3,1,0:T(8,128)S(1)}, u32[]{:S(2)}, u32[]{:S(2)}) async-start(f32[16,2,128,128]{2,3,1,0:T(8,128)} %bitcast.18), calls=%async_computation.1 | async-start | bytes 4194304 | tf_op jit(solution)/shard_map/all_to_all | solution.py:62
  220.4 12.7 %copy-start.3 = (s32[192]{0:T(256)S(1)}, s32[192]{0:T(256)}, u32[]{:S(2)}) copy-start(s32[192]{0:T(256)} %param.15) | copy-start | bytes 2308
  242.7 3.8 %copy-start.1 = (f32[32,128,128]{2,1,0:T(8,128)S(1)}, f32[32,128,128]{2,1,0:T(8,128)}, u32[]{:S(2)}) copy-start(f32[32,128,128]{2,1,0:T(8,128)} %param.16) | copy-start | bytes 6291460
Sparse Core Ops, SparseCore 0:
  9.5 114.3 all-gather.1
where the time goes:
time: 254 us; the launch traced here: 253 us
  waiting for transfers between devices  106 us (42%)
  local copies, waits for them, and re-layouts  60.1 us (24%)
  matrix products  51.8 us (20%)
  starting transfers between devices  19.2 us (8%)
  between operations  13.5 us (5%)
  other arithmetic  2.63 us (1%)
    all_gather x1, waiting for transfers between devices, local(): group = lax.all_gather(sims, 'nbr', axis=0, tiled=True)  105 us
    gather x6, local copies, waits for them, and re-layouts, pick_from(): taken = jnp.take(source, jnp.clip(index, 0, length - 1), axis=0)  40.1 us
    dot_general x1, matrix products, local(): own_terms = jnp.einsum('tij,tjs->tis', own_tiles, own_pick, precision=high)  33.9 us
    dot_general x1, local copies, waits for them, and re-layouts, local(): own_terms = jnp.einsum('tij,tjs->tis', own_tiles, own_pick, precision=high)  12.7 us
    all_to_all x1, starting transfers between devices, local(): lax.all_to_all(out_rows, 'nbr', split_axis=0, concat_axis=0, tiled=True)  8.42 us
    dot_general x1, matrix products, local(): jnp.einsum('tij,tjs->tis', help_tiles, help_pick, precision=high)  8.31 us
    dot_general x1, matrix products, local(): own_sum = jnp.einsum('rt,tis->ris', select, own_terms, precision=high)  7.07 us
  transfers between devices with their start and end apart: 5, of which 1 were waited for; matrix products, arithmetic and copies ran while one was open for 38% of the time, Pallas kernels for 0%

commit v1 on v0

--- a/solution.py
+++ b/solution.py
@@ -4,6 +4,15 @@
 from jax.sharding import PartitionSpec as P
 
 RIM = 8
+
+
+def forms_clear(mat):
+    return jnp.concatenate(
+        lax.all_to_all(
+            jnp.stack([mat] * lax.axis_size("nbr")), axis_name="nbr", concat_axis=0, split_axis=0
+        ),
+        axis=0,
+    )
 
 
 def padded(shard, sides, width):
@@ -34,7 +43,7 @@
     group_rows = rows_dev * neighbours
     help_dev = help_tiles.shape[0]
     slots_owner = help_dev // neighbours
-    group = lax.all_gather(sims, "nbr", axis=0, tiled=True)
+    group = forms_clear(sims)
     own_pick = pick_from(group, RIM, own_cols)
     help_pick = pick_from(group, RIM, help_cols)
     edges = jnp.concatenate([group[:RIM], group[group_rows - RIM :]], axis=0)

time: 254 us -> 448 us (1.76)
  waiting for transfers between devices: 106 us -> 293 us
  starting transfers between devices: 19.2 us -> 32.7 us
  between operations: 13.5 us -> 0.18 us
  local copies, waits for them, and re-layouts: 60.1 us -> 69.6 us
    all_to_all x0 -> x1, waiting for transfers between devices: none -> 293 us  [forms_clear(): lax.all_to_all(jnp.stack([mat] * lax.axis_size('nbr')), axis_name='nbr',...]
    all_gather x1 -> x0, waiting for transfers between devices: 105 us -> none  [local(): group = lax.all_gather(sims, 'nbr', axis=0, tiled=True)]
    another operation x0 -> x1, local copies, waits for them, and re-layouts: none -> 9.35 us  [forms_clear(): jnp.stack([mat] * lax.axis_size('nbr'))]
    all_to_all x0 -> x1, starting transfers between devices: none -> 8.61 us  [forms_clear(): lax.all_to_all(jnp.stack([mat] * lax.axis_size('nbr')), axis_name='nbr',...]
  transfers between devices with their start and end apart: 5 -> 5, of which waited for: 1 -> 1; matrix products, arithmetic and copies ran while one was open for 38% -> 21% of each run, Pallas kernels for 0% -> 0%
where the time goes in v1:
time: 448 us
  waiting for transfers between devices  293 us (65%)
  local copies, waits for them, and re-layouts  69.6 us (16%)
  matrix products  51.8 us (12%)
  starting transfers between devices  32.7 us (7%)
    all_to_all x1, waiting for transfers between devices, forms_clear(): lax.all_to_all(jnp.stack([mat] * lax.axis_size('nbr')), axis_name='nbr',...  293 us
    gather x6, local copies, waits for them, and re-layouts, pick_from(): taken = jnp.take(source, jnp.clip(index, 0, length - 1), axis=0)  40.1 us
    dot_general x1, matrix products, local(): own_terms = jnp.einsum('tij,tjs->tis', own_tiles, own_pick, precision=high)  33.9 us
    dot_general x1, local copies, waits for them, and re-layouts, local(): own_terms = jnp.einsum('tij,tjs->tis', own_tiles, own_pick, precision=high)  12.8 us
    all_to_all x1, starting transfers between devices, local(): lax.all_to_all(out_rows, 'nbr', split_axis=0, concat_axis=0, tiled=True)  9.95 us
    another operation x1, local copies, waits for them, and re-layouts, forms_clear(): jnp.stack([mat] * lax.axis_size('nbr'))  9.35 us
  transfers between devices with their start and end apart: 5, of which 1 were waited for; matrix products, arithmetic and copies ran while one was open for 21% of the time, Pallas kernels for 0%

profile of v1, /device:TPU:1, one launch (start us, length us, event | category | flops | bytes accessed | tf_op | source)
XLA Modules:
  0.0 447.6 jit_solution(10361106851248171014)
XLA Ops:
  0.0 0.0 copy-start
  0.0 9.4 %stack.2 = f32[16,16,128,128]{3,2,1,0:T(8,128)} broadcast(f32[16,128,128]{2,1,0:T(8,128)} %param.12), dimensions={1,2,3} | broadcast | bytes 17825792 | tf_op jit(solution)/shard_map/stack | solution.py:12
  9.4 0.0 copy-start.5
  9.4 0.0 copy-start.2
  9.4 0.0 copy-start.4
  9.4 0.0 copy-start.6
  9.4 8.6 %all-to-all-start = ((f32[16,16,128,128]{3,2,1,0:T(8,128)}), f32[16,16,128,128]{3,2,1,0:T(8,128)}, u32[]{:S(2)}, u32[]{:S(2)}) async-start(f32[16,16,128,128]{3,2,1,0:T(8,128)} %stack.2), calls=%async_computation | async-start | bytes 33554432 | tf_op jit(solution)/shard_map/all_to_all | solution.py:11
  18.0 0.0 copy-done.5
  18.0 0.7 all_to_all.13
  18.7 0.0 copy-done.2
  18.7 0.0 copy-done.4
  18.7 292.6 %all-to-all-done = f32[16,16,128,128]{3,2,1,0:T(8,128)} async-done(((f32[16,16,128,128]{3,2,1,0:T(8,128)}), f32[16,16,128,128]{3,2,1,0:T(8,128)}, u32[]{:S(2)}, u32[]{:S(2)}) %all-to-all-start) | async-done | bytes 16777248 | tf_op jit(solution)/shard_map/all_to_all | solution.py:11
  311.3 9.9 %all-to-all-start.1 = ((f32[16,1,2]{2,1,0:T(1,128)}), f32[16,1,2]{2,1,0:T(1,128)S(1)}, u32[]{:S(2)}, u32[]{:S(2)}) async-start(f32[16,1,2]{2,1,0:T(1,128)} %bitcast.3), calls=%async_computation.1 | async-start | bytes 16384 | tf_op jit(solution)/shard_map/all_to_all | solution.py:72
  321.3 2.3 fusion.43
  323.5 5.3 %collective-permute-start = (f32[8,128,128]{2,1,0:T(8,128)}, f32[8,128,128]{2,1,0:T(8,128)S(1)}, u32[]{:S(2)}, u32[]{:S(2)}) collective-permute-start(f32[8,128,128]{2,1,0:T(8,128)} %get-tuple-element.17), channel_id=1, source_target_pairs={{0,16},{16,32},{32,48},{48,64},{64,80},{80,96},{96,112},{1,17},{17... | collective-permute-start | bytes 1572872 | tf_op jit(solution)/shard_map/ppermute | solution.py:25
  328.8 1.9 collective-permute-start.1
  330.8 0.0 copy-done.6
  330.8 0.0 all-to-all-done.1
  330.8 0.5 broadcast.84
  331.4 0.7 reduce.3
  332.0 0.1 eq.31
  332.1 7.8 %gather_fusion.1 = f32[32,128,128]{2,1,0:T(8,128)} fusion(f32[256,128,128]{2,1,0:T(8,128)} %bitcast.1, s32[1024]{0:T(1024)S(1)} %pad_clamp_fusion.2), kind=kCustom, calls=%fused_computation.5 | custom fusion | bytes 4194432 | tf_op jit(solution)/shard_map/jit(_take)/gather | solution.py:35
  339.9 16.5 %gather_fusion = f32[192,128,128]{2,1,0:T(8,128)} fusion(f32[256,128,128]{2,1,0:T(8,128)} %bitcast.1, s32[1024]{0:T(1024)S(1)} %get-tuple-element.37), kind=kCustom, calls=%fused_computation.4 | custom fusion | bytes 25166592 | tf_op jit(solution)/shard_map/jit(_take)/gather | solution.py:35
  356.4 0.0 collective-permute-done.1
  356.4 2.0 gather_fusion.5
  358.4 0.0 collective-permute-done
  358.4 2.0 gather_fusion.4
  360.4 0.0 copy-done
  360.4 8.3 %fusion.24 = f32[32,128,128]{2,1,0:T(8,128)} fusion(f32[32,128,128]{2,1,0:T(8,128)S(1)} %copy-done, f32[32,128,128]{2,1,0:T(8,128)} %gather_fusion.5, f32[32,128,128]{2,1,0:T(8,128)} %gather_fusion.4, f32[32,128,128]{2,1,0:T(8,128)} %gather_fusion.1, f32[32]{0:T(128)S(1)} %convert_element_type.33, f32[32]{0:T(128)S(1)} %get-tuple-element.28, ...), kind=kOutput, calls=%fused_computation.28 | convolution fusion | flops 810024960 | bytes 10486368 | tf_op jit(solution)/shard_map/tij,tjs->tis/dot_general | solution.py:65
  368.7 6.9 %all-to-all-start.2 = ((f32[16,2,128,128]{2,3,1,0:T(8,128)}), f32[16,2,128,128]{2,3,1,0:T(8,128)S(1)}, u32[]{:S(2)}, u32[]{:S(2)}) async-start(f32[16,2,128,128]{2,3,1,0:T(8,128)} %bitcast.19), calls=%async_computation.2 | async-start | bytes 4194304 | tf_op jit(solution)/shard_map/all_to_all | solution.py:71
  375.7 5.9 %gather_fusion.2 = f32[192,128,128]{2,1,0:T(8,128)} fusion(f32[8,128,128]{2,1,0:T(8,128)S(1)} %collective-permute-done, s32[1024]{0:T(1024)S(1)} %pad_clamp_fusion.4), kind=kCustom, calls=%fused_computation.clone | custom fusion | bytes 25166592 | tf_op jit(solution)/shard_map/jit(_take)/gather | solution.py:35
  381.6 5.9 %gather_fusion.3 = f32[192,128,128]{2,1,0:T(8,128)} fusion(f32[8,128,128]{2,1,0:T(8,128)S(1)} %collective-permute-done.1, s32[1024]{0:T(1024)S(1)} %get-tuple-element.36), kind=kCustom, calls=%fused_computation.2.clone | custom fusion | bytes 25166592 | tf_op jit(solution)/shard_map/jit(_take)/gather | solution.py:35
  387.5 33.9 %fusion.14 = f32[192,128,128]{1,2,0:T(8,128)} fusion(f32[192,128,128]{2,1,0:T(8,128)} %param.13, f32[192,128,128]{2,1,0:T(8,128)} %gather_fusion.3, f32[192,128,128]{2,1,0:T(8,128)} %gather_fusion.2, f32[192,128,128]{2,1,0:T(8,128)} %gather_fusion, f32[192]{0:T(256)S(1)} %get-tuple-element.21, f32[192]{0:T(256)S(1)} %get-tuple-element.26, ...), kind=kOutput, calls=%fused_computation.20 | convolution fusion | flops 4857004032 | bytes 62917440 | tf_op jit(solution)/shard_map/tij,tjs->tis/dot_general | solution.py:59
  421.4 0.0 copy-start.3
  421.4 12.8 %copy.15 = f32[192,128,128]{2,0,1:T(8,128)} copy(f32[192,128,128]{1,2,0:T(8,128)} %fusion.14) | data formatting | bytes 25165824 | tf_op jit(solution)/shard_map/tij,tjs->tis/dot_general | solution.py:59
  434.1 0.0 copy-done.3
  434.1 7.1 %fusion.35 = f32[16,128,128]{2,0,1:T(8,128)S(1)} fusion(f32[192,128,128]{2,0,1:T(8,128)} %copy.15, s32[192]{0:T(256)S(1)} %copy-done.3), kind=kOutput, calls=%fused_computation.39 | convolution fusion | flops 603982848 | bytes 13632256 | tf_op jit(solution)/shard_map/rt,tis->ris/dot_general | solution.py:63
  441.2 0.0 all-to-all-done.2
  441.2 2.5 copy.18
  443.7 0.0 copy-start.1
  443.7 2.5 convolution_add_fusion
  446.3 1.3 copy.19
  447.5 0.0 copy-done.1
  (9 shorter events, 0.1 us)
Async XLA Ops:
  0.0 360.4 %copy-start = (f32[32,128,128]{2,1,0:T(8,128)S(1)}, f32[32,128,128]{2,1,0:T(8,128)}, u32[]{:S(2)}) copy-start(f32[32,128,128]{2,1,0:T(8,128)} %param.16) | copy-start | bytes 6291460
  9.4 8.6 %copy-start.5 = (s32[32]{0:T(128)S(1)}, s32[32]{0:T(128)}, u32[]{:S(2)}) copy-start(s32[32]{0:T(128)} %param.18) | copy-start | bytes 388
  9.4 9.3 %copy-start.2 = (s32[192]{0:T(256)S(1)}, s32[192]{0:T(256)}, u32[]{:S(2)}) copy-start(s32[192]{0:T(256)} %param.14) | copy-start | bytes 2308
  9.4 9.4 %copy-start.4 = (s32[32]{0:T(128)S(1)}, s32[32]{0:T(128)}, u32[]{:S(2)}) copy-start(s32[32]{0:T(128)} %param.17) | copy-start | bytes 388
  9.4 321.4 %copy-start.6 = (s32[32]{0:T(128)S(1)}, s32[32]{0:T(128)}, u32[]{:S(2)}) copy-start(s32[32]{0:T(128)} %param.19) | copy-start | bytes 388
  9.4 301.9 %all-to-all-start = ((f32[16,16,128,128]{3,2,1,0:T(8,128)}), f32[16,16,128,128]{3,2,1,0:T(8,128)}, u32[]{:S(2)}, u32[]{:S(2)}) async-start(f32[16,16,128,128]{3,2,1,0:T(8,128)} %stack.2), calls=%async_computation | async-start | bytes 33554432 | tf_op jit(solution)/shard_map/all_to_all | solution.py:11
  311.3 19.5 %all-to-all-start.1 = ((f32[16,1,2]{2,1,0:T(1,128)}), f32[16,1,2]{2,1,0:T(1,128)S(1)}, u32[]{:S(2)}, u32[]{:S(2)}) async-start(f32[16,1,2]{2,1,0:T(1,128)} %bitcast.3), calls=%async_computation.1 | async-start | bytes 16384 | tf_op jit(solution)/shard_map/all_to_all | solution.py:72
  323.5 34.9 %collective-permute-start = (f32[8,128,128]{2,1,0:T(8,128)}, f32[8,128,128]{2,1,0:T(8,128)S(1)}, u32[]{:S(2)}, u32[]{:S(2)}) collective-permute-start(f32[8,128,128]{2,1,0:T(8,128)} %get-tuple-element.17), channel_id=1, source_target_pairs={{0,16},{16,32},{32,48},{48,64},{64,80},{80,96},{96,112},{1,17},{17... | collective-permute-start | bytes 1572872 | tf_op jit(solution)/shard_map/ppermute | solution.py:25
  328.8 27.6 %collective-permute-start.1 = (f32[8,128,128]{2,1,0:T(8,128)}, f32[8,128,128]{2,1,0:T(8,128)S(1)}, u32[]{:S(2)}, u32[]{:S(2)}) collective-permute-start(f32[8,128,128]{2,1,0:T(8,128)} %get-tuple-element.18), channel_id=1, source_target_pairs={{16,0},{32,16},{48,32},{64,48},{80,64},{96,80},{112,96},{17,1},{33... | collective-permute-start | bytes 1572872 | tf_op jit(solution)/shard_map/ppermute | solution.py:26
  368.7 72.5 %all-to-all-start.2 = ((f32[16,2,128,128]{2,3,1,0:T(8,128)}), f32[16,2,128,128]{2,3,1,0:T(8,128)S(1)}, u32[]{:S(2)}, u32[]{:S(2)}) async-start(f32[16,2,128,128]{2,3,1,0:T(8,128)} %bitcast.19), calls=%async_computation.2 | async-start | bytes 4194304 | tf_op jit(solution)/shard_map/all_to_all | solution.py:71
  421.4 12.8 %copy-start.3 = (s32[192]{0:T(256)S(1)}, s32[192]{0:T(256)}, u32[]{:S(2)}) copy-start(s32[192]{0:T(256)} %param.15) | copy-start | bytes 2308
  443.7 3.8 copy-start.1
